TPU v7x, 128 devices: a whole 4x4x4 slice. The times are simulated.
128 devices in a mesh: tok: 8 (over y, x_lo), tp: 16 (over z, x_hi, core).
Axes of the slice: x: 4 (x_hi: 2, x_lo: 2; x = x_hi * 2 + x_lo), y: 4, z: 4, core: 2. Of those that a mesh axis runs over, the one named last changes fastest.
Arguments:
- source: bfloat16 [2048, 8192], P('tp', 'tok'), may hold values from -6 to 6
- row_token: int32 [2048], replicated, may hold values from 0 to 2047, each once
- seg_ids: int32 [8, 256], P('tok'), may hold values from 0 to 3, never falling along the last dimension, each value on 1 to 128 neighbouring positions
- stitch_weight: bfloat16 [8192, 8192], P('tok', 'tp'), may hold values from -0.0625 to 0.0625
- norm_gain: float32 [8192], replicated, may hold values from 0.5 to 1.5
- q_weight: bfloat16 [8192, 8192], P(None, 'tp'), may hold values from -2 to 2
- kv_weight: bfloat16 [8192, 2048], P(None, 'tp'), may hold values from -2 to 2
- o_weight: bfloat16 [8192, 8192], P('tp'), may hold values from -0.0625 to 0.0625
- out_grad: bfloat16 [2048, 8192], P('tok', 'tp'), may hold values from -6 to 6
Outputs:
- layer_out: bfloat16 [2048, 8192], P('tok', 'tp')
- stitch_grad: float32 [8192, 8192], P('tok', 'tp')
Inputs may be any that keep to these rules, and one draw needn't show every extreme that they name: `row_token`: each token index appears exactly once. `seg_ids`: within a pack the ids never fall; a document holds 1 to 128 tokens.
All inputs are finite; a program needn't handle non-finite values.
Results may differ from a plain program's by a relative error of at most 0.024.
Values may be sent and summed in bfloat16 or wider, within the bound.
A program may use at most 128 MiB of HBM per device.

v0:
```python
import math
import jax
import jax.numpy as jnp
from jax import lax
from jax.sharding import PartitionSpec as P

HD = 128
epsilon = 1e-05


def swapped(value, axis, distance):
    mask = 2**distance
    pairs = [(source, source ^ mask) for source in range(lax.axis_size(axis))]
    return lax.ppermute(value, axis, pairs)


def frequencies():
    exponent = jnp.arange(0, HD, 2).astype(jnp.float32) / HD
    plain_rate = 500000.0 ** (-exponent)
    wavelength = 2.0 * math.pi / plain_rate
    smoothing = (8192.0 / wavelength - 1.0) / 3.0
    blended = (1.0 - smoothing) * plain_rate / 8.0 + smoothing * plain_rate
    return jnp.where(
        wavelength < 2048.0, plain_rate, jnp.where(wavelength > 8192.0, plain_rate / 8.0, blended)
    )


def rotate(vector_in, cosine_table, sine_table):
    half_size = vector_in.shape[-1] // 2
    first_half = vector_in[..., :half_size]
    second = vector_in[..., half_size:]
    return jnp.concatenate(
        [
            first_half * cosine_table - second * sine_table,
            second * cosine_table + first_half * sine_table,
        ],
        axis=-1,
    )


def unrotate(vector_in, cosine_table, sine_table):
    half_size = vector_in.shape[-1] // 2
    first_half = vector_in[..., :half_size]
    second = vector_in[..., half_size:]
    return jnp.concatenate(
        [
            first_half * cosine_table + second * sine_table,
            second * cosine_table - first_half * sine_table,
        ],
        axis=-1,
    )


def body(
    source, row_token, seg_ids, stitch_weight, norm_gain, q_weight, kv_weight, o_weight, out_grad
):
    tp_rank = lax.axis_index("tp")
    pack_len = seg_ids.shape[1]
    score_scale = 1.0 / math.sqrt(HD)
    gathered = lax.all_gather(source, "tp", axis=0, tiled=True)
    every_row_stack = gathered.shape[0]
    placing = (
        jnp.zeros((every_row_stack,), jnp.int32)
        .at[row_token]
        .set(jnp.arange(every_row_stack, dtype=jnp.int32))
    )
    column_block = jnp.take(gathered, placing, axis=0)
    token_rows = lax.all_to_all(column_block, "tok", split_axis=0, concat_axis=1, tiled=True)
    features = token_rows
    hidden_cols = jnp.dot(
        features,
        lax.all_gather(stitch_weight, "tok", axis=0, tiled=True),
        preferred_element_type=jnp.float32,
    )
    hidden_bf = hidden_cols.astype(jnp.bfloat16)
    hidden_all = lax.all_gather(hidden_bf, "tp", axis=1, tiled=True)
    hidden_f = hidden_all.astype(jnp.float32)
    inv_rms = lax.rsqrt(jnp.mean(hidden_f * hidden_f, axis=1, keepdims=True) + epsilon)
    normed = (hidden_f * inv_rms * norm_gain).astype(jnp.bfloat16)
    seg_row = seg_ids[0]
    earlier = jnp.sum((seg_row[None, :] < seg_row[:, None]).astype(jnp.int32), axis=1)
    index_row = jnp.arange(pack_len, dtype=jnp.int32)
    angles = (index_row - earlier).astype(jnp.float32)[:, None] * frequencies()[None, :]
    cosines = jnp.cos(angles)[:, None, :]
    sine_table = jnp.sin(angles)[:, None, :]
    allowed = (
        (seg_row[:, None] == seg_row[None, :]) & (index_row[None, :] <= index_row[:, None])
    ).astype(jnp.int32)
    local_heads = q_weight.shape[1] // HD
    kv_local = 1
    repeat = local_heads // kv_local
    queries = rotate(
        jnp.dot(normed, q_weight, preferred_element_type=jnp.float32).reshape(
            pack_len, local_heads, HD
        ),
        cosines,
        sine_table,
    ).astype(jnp.bfloat16)
    projected = jnp.dot(normed, kv_weight, preferred_element_type=jnp.float32)
    is_key = tp_rank % 2 == 0
    own_part = jnp.where(
        is_key, rotate(projected, cosines[:, 0], sine_table[:, 0]), projected
    ).astype(jnp.bfloat16)
    partner = swapped(own_part, "tp", 0)
    per_head_keys = jnp.where(is_key, own_part, partner)[:, None, :]
    per_head_values = jnp.where(is_key, partner, own_part)[:, None, :]
    per_head_queries = queries.reshape(pack_len, kv_local, repeat, HD)
    scores = (
        jnp.einsum(
            "nkej,wkj->kenw", per_head_queries, per_head_keys, preferred_element_type=jnp.float32
        )
        * score_scale
    )
    scores = jnp.where(allowed != 0, scores, -1e30)
    row_max = jnp.max(scores, axis=-1, keepdims=True)
    exponents = jnp.exp(scores - row_max)
    attention = exponents / jnp.sum(exponents, axis=-1, keepdims=True)
    attention_half_precision = attention.astype(jnp.bfloat16)
    context = jnp.einsum(
        "cnfo,och->fcnh",
        attention_half_precision,
        per_head_values,
        preferred_element_type=jnp.float32,
    ).astype(jnp.bfloat16)
    context = context.reshape(pack_len, local_heads * HD)
    attended = lax.psum_scatter(
        jnp.dot(context, o_weight, preferred_element_type=jnp.float32).astype(jnp.bfloat16),
        "tp",
        scatter_dimension=1,
        tiled=True,
    ).astype(jnp.float32)
    layer_out = (hidden_bf.astype(jnp.float32) + attended).astype(jnp.bfloat16)
    gradient_every_row = lax.all_gather(out_grad, "tp", axis=1, tiled=True)
    grad_context = jnp.dot(
        gradient_every_row, o_weight.T, preferred_element_type=jnp.float32
    ).astype(jnp.bfloat16)
    context_gradient = grad_context.reshape(pack_len, kv_local, repeat, HD)
    grad_probs = jnp.einsum(
        "nkej,wkj->kenw", context_gradient, per_head_values, preferred_element_type=jnp.float32
    )
    centered = grad_probs - jnp.sum(grad_probs * attention, axis=-1, keepdims=True)
    score_gradient = (attention * centered * score_scale).astype(jnp.bfloat16)
    query_grad = jnp.einsum(
        "cnfo,och->fcnh", score_gradient, per_head_keys, preferred_element_type=jnp.float32
    )
    grad_queries = unrotate(
        query_grad.reshape(pack_len, local_heads, HD), cosines, sine_table
    ).astype(jnp.bfloat16)
    key_part = jnp.einsum(
        "bwlf,lbwj->fbj", score_gradient, per_head_queries, preferred_element_type=jnp.float32
    )
    value_part = jnp.einsum(
        "bwlf,lbwj->fbj",
        attention_half_precision,
        context_gradient,
        preferred_element_type=jnp.float32,
    )
    outgoing = jnp.where(is_key, value_part, key_part)[:, 0]
    incoming = swapped(outgoing.astype(jnp.bfloat16), "tp", 0).astype(outgoing.dtype)
    own_sum = jnp.where(is_key, key_part, value_part)[:, 0] + incoming
    grad_pairs = jnp.where(
        is_key, unrotate(own_sum, cosines[:, 0], sine_table[:, 0]), own_sum
    ).astype(jnp.bfloat16)
    grad_normed = jnp.dot(
        grad_queries.reshape(pack_len, local_heads * HD),
        q_weight.T,
        preferred_element_type=jnp.float32,
    )
    grad_normed = grad_normed + jnp.dot(grad_pairs, kv_weight.T, preferred_element_type=jnp.float32)
    weighted = norm_gain * grad_normed
    cubed = inv_rms * inv_rms * inv_rms
    norm_term = inv_rms * weighted - hidden_f * cubed * jnp.mean(
        weighted * hidden_f, axis=1, keepdims=True
    )
    grad_sum = lax.psum_scatter(
        norm_term.astype(jnp.bfloat16), "tp", scatter_dimension=1, tiled=True
    ).astype(jnp.float32)
    grad_hidden = (out_grad.astype(jnp.float32) + grad_sum).astype(jnp.bfloat16)
    features = token_rows
    stitch_grad = lax.psum_scatter(
        lax.dot_general(
            features, grad_hidden, (((0,), (0,)), ((), ())), preferred_element_type=jnp.float32
        ).astype(jnp.bfloat16),
        "tok",
        scatter_dimension=0,
        tiled=True,
    ).astype(jnp.float32)
    return (layer_out, stitch_grad)


def solution(mesh):
    placed = (
        P("tp", "tok"),
        P(),
        P("tok", None),
        P("tok", "tp"),
        P(),
        P(None, "tp"),
        P(None, "tp"),
        P("tp", None),
        P("tok", "tp"),
    )
    return jax.shard_map(
        body,
        mesh=mesh,
        in_specs=placed,
        out_specs=(P("tok", "tp"), P("tok", "tp")),
        check_vma=False,
    )
```

profile of v0, /device:TPU:1, one launch (start us, length us, event | category | flops | bytes accessed | tf_op | source)
XLA Modules:
  0.0 783.7 jit_solution(5317935610867189701)
XLA Ops:
  10.1 8.0 %scatter_custom_fusion = s32[2048]{0:T(1024)S(1)} fusion(s32[2048]{0:T(1024)S(1)} %compare_select_fusion.1, s32[2048]{0:T(1024)S(1)} %iota.19, s32[]{:T(128)} %constant.22.clone.1), kind=kCustom, calls=%fused_computation.84 | custom fusion | bytes 8196 | tf_op jit(solution)/shard_map/scatter | solution.py:65
  18.2 51.3 %all-gather.5.cloned.1.call-done = bf16[2048,1024]{1,0:T(8,128)(2,1)} async-done(((bf16[128,1024]{1,0:T(8,128)(2,1)}), bf16[2048,1024]{1,0:T(8,128)(2,1)}) %all-gather.5.cloned.1.call-update) | async-done | bytes 4194320 | tf_op jit(solution)/shard_map/all_gather | solution.py:60
  69.6 13.6 %gather_fusion = bf16[2048,1024]{1,0:T(8,128)(2,1)} fusion(bf16[2048,1024]{1,0:T(8,128)(2,1)} %all-gather.5.cloned.1.call-done, s32[2048]{0:T(1024)S(1)} %fusion.43), kind=kCustom, calls=%fused_computation | custom fusion | bytes 8396800 | tf_op jit(solution)/shard_map/jit(_take)/gather | solution.py:67
  83.2 6.4 copy.25
  89.7 2.6 broadcast_select_fusion
  92.3 98.4 %all_to_all.16 = bf16[8,256,1024]{1,2,0:T(8,128)(2,1)} all-to-all(bf16[8,256,1024]{1,2,0:T(8,128)(2,1)S(1)} %broadcast_select_fusion), channel_id=1, replica_groups=mesh['tok'=8,'tp'=16] {'tok'}, dimensions={0} | all-to-all | bytes 8388608 | tf_op jit(solution)/shard_map/all_to_all | solution.py:68
  190.7 91.1 %all-gather.7.cloned.1.call-done = bf16[8192,512]{1,0:T(8,128)(2,1)} async-done(((bf16[1024,512]{1,0:T(8,128)(2,1)}), bf16[8192,512]{1,0:T(8,128)(2,1)}) %all-gather.7.cloned.1.call-update) | async-done | bytes 8388624 | tf_op jit(solution)/shard_map/all_gather | solution.py:72
  281.8 7.7 convolution_convert_fusion.4
  291.0 51.5 %all-gather.11.cloned.1.call-done = bf16[256,8192]{1,0:T(8,128)(2,1)} async-done(((bf16[256,512]{1,0:T(8,128)(2,1)}), bf16[256,8192]{1,0:T(8,128)(2,1)}) %all-gather.11.cloned.1.call-update) | async-done | bytes 4194320 | tf_op jit(solution)/shard_map/all_gather | solution.py:133
  342.6 7.0 convolution_convert_fusion.3
  350.4 49.4 %all-gather.9.cloned.1.call-done = bf16[256,8192]{1,0:T(8,128)(2,1)} async-done(((bf16[256,512]{1,0:T(8,128)(2,1)}), bf16[256,8192]{1,0:T(8,128)(2,1)}) %all-gather.9.cloned.1.call-update) | async-done | bytes 4194320 | tf_op jit(solution)/shard_map/all_gather | solution.py:76
  399.9 3.3 fusion.1
  403.7 3.9 fusion.12
  408.5 5.8 fusion.10
  416.5 1.9 convolution_bitcast_fusion.2
  424.2 5.9 fusion.53
  430.6 5.3 fusion.7
  435.9 5.9 fusion.6
  442.4 7.7 convolution_convert_fusion.1
  450.3 68.1 %reduce-scatter.6.cloned.1.call-done = bf16[256,512]{1,0:T(8,128)(2,1)} async-done(((bf16[256,8192]{1,0:T(8,128)(2,1)}), bf16[256,512]{1,0:T(8,128)(2,1)}) %reduce-scatter.6.cloned.1.call-update) | async-done | bytes 262160 | tf_op jit(solution)/shard_map/reduce_scatter | solution.py:175
  518.4 7.8 convolution_convert_fusion
  526.2 76.0 %reduce-scatter.4.cloned.1.call-done = bf16[256,512]{1,0:T(8,128)(2,1)} async-done(((bf16[256,8192]{1,0:T(8,128)(2,1)}), bf16[256,512]{1,0:T(8,128)(2,1)}) %reduce-scatter.4.cloned.1.call-update) | async-done | bytes 262160 | tf_op jit(solution)/shard_map/reduce_scatter | solution.py:126
  604.0 170.1 %reduce-scatter.8.cloned.1.call-done = bf16[1024,512]{1,0:T(8,128)(2,1)} async-done(((bf16[8192,512]{1,0:T(8,128)(2,1)}), bf16[1024,512]{1,0:T(8,128)(2,1)}) %reduce-scatter.8.cloned.1.call-update) | async-done | bytes 1048592 | tf_op jit(solution)/shard_map/reduce_scatter | solution.py:180
  774.0 2.8 convert_element_type.137
  (86 shorter events, 17.3 us)
Async XLA Ops:
  7.2 396.5 %copy-start = (bf16[8192,128]{1,0:T(8,128)(2,1)S(1)}, bf16[8192,128]{1,0:T(8,128)(2,1)}, u32[]{:S(2)}) copy-start(bf16[8192,128]{1,0:T(8,128)(2,1)} %param.15) | copy-start | bytes 6291460
  7.2 62.4 %all-gather.5.cloned.1.call-start = ((), (), s32[]{:S(2)}) async-start(), calls=%async_computation.4 | async-start | bytes 4456448 | tf_op jit(solution)/shard_map/all_gather | solution.py:60
  7.9 273.9 %all-gather.7.cloned.1.call-start = ((), (), s32[]{:S(2)}) async-start(), calls=%async_computation.5 | async-start | bytes 9437184 | tf_op jit(solution)/shard_map/all_gather | solution.py:72
  8.7 333.9 %all-gather.11.cloned.1.call-start = ((), (), s32[]{:S(2)}) async-start(), calls=%async_computation.8 | async-start | bytes 4456448 | tf_op jit(solution)/shard_map/all_gather | solution.py:133
  9.4 390.5 %all-gather.9.cloned.1.call-start = ((), (), s32[]{:S(2)}) async-start(), calls=%async_computation.6 | async-start | bytes 4456448 | tf_op jit(solution)/shard_map/all_gather | solution.py:76
  281.8 7.8 copy-start.13
  289.6 228.8 %reduce-scatter.6.cloned.1.call-start = ((), (), s32[]{:S(2)}) async-start(), calls=%async_computation.9 | async-start | bytes 4456448 | tf_op jit(solution)/shard_map/reduce_scatter | solution.py:175
  291.0 112.6 %copy-start.11 = (f32[8192]{0:T(1024)S(1)}, f32[8192]{0:T(1024)}, u32[]{:S(2)}) copy-start(f32[8192]{0:T(1024)} %param.13) | copy-start | bytes 98308
  399.9 8.6 %copy-start.1 = (bf16[256,8192]{1,0:T(8,128)(2,1)S(1)}, bf16[256,8192]{1,0:T(8,128)(2,1)}, u32[]{:S(2)}) copy-start(bf16[256,8192]{1,0:T(8,128)(2,1)} %all-gather.9.cloned.1.call-done) | copy-start | bytes 12582916
  403.7 10.6 %copy-start.15 = (f32[256]{0:T(256)}, f32[256]{0:T(256)S(1)}, u32[]{:S(2)}) copy-start(f32[256]{0:T(256)S(1)} %get-tuple-element.15) | copy-start | bytes 3076
  408.0 10.5 %copy-start.5 = (bf16[256,128]{0,1:T(8,128)(2,1)}, bf16[256,128]{0,1:T(8,128)(2,1)S(1)}, u32[]{:S(2)}) copy-start(bf16[256,128]{0,1:T(8,128)(2,1)S(1)} %fusion.22) | copy-start | bytes 196612
  408.0 7.0 collective-permute-start
  423.0 7.2 collective-permute-start.1
  424.2 6.0 copy-start.7
  424.2 6.3 copy-start.2
  424.2 6.3 copy-start.12
  430.6 5.3 copy-start.14
  430.6 5.3 copy-start.16
  435.9 6.2 copy-start.6
  435.9 6.2 copy-start.10
  441.8 160.5 %reduce-scatter.4.cloned.1.call-start = ((), (), s32[]{:S(2)}) async-start(), calls=%async_computation.7 | async-start | bytes 4456448 | tf_op jit(solution)/shard_map/reduce_scatter | solution.py:126
  442.4 76.0 %copy-start.4 = (bf16[256,512]{1,0:T(8,128)(2,1)S(1)}, bf16[256,512]{1,0:T(8,128)(2,1)}, u32[]{:S(2)}) copy-start(bf16[256,512]{1,0:T(8,128)(2,1)} %param.17) | copy-start | bytes 786436
  450.2 152.0 %copy-start.3 = (bf16[256,512]{1,0:T(8,128)(2,1)S(1)}, bf16[256,512]{1,0:T(8,128)(2,1)}, u32[]{:S(2)}) copy-start(bf16[256,512]{1,0:T(8,128)(2,1)} %convolution_convert_fusion.4) | copy-start | bytes 786436
  450.2 323.8 %reduce-scatter.8.cloned.1.call-start = ((), (), s32[]{:S(2)}) async-start(), calls=%async_computation.10 | async-start | bytes 9437184 | tf_op jit(solution)/shard_map/reduce_scatter | solution.py:180
  (2 other events, 7.7 us)
Sparse Core Ops, SparseCore 0:
  10.5 59.0 all-gather.4
  71.2 210.5 all-gather.6
  284.2 58.3 all-gather.10
  345.3 54.5 all-gather.8
  441.9 76.4 reduce-scatter.5
  522.8 79.4 reduce-scatter.3
  604.6 169.3 reduce-scatter.7
where the time goes:
time: 784 us
  waiting for transfers between devices  560 us (71%)
  blocking collectives  98.4 us (13%)
  matrix products  56.8 us (7%)
  local copies, waits for them, and re-layouts  30.8 us (4%)
  other arithmetic  21.2 us (3%)
  between operations  14.5 us (2%)
    reduce_scatter x1, waiting for transfers between devices, body(): lax.psum_scatter(lax.dot_general(features, grad_hidden, (((0,), (0,)), ((...  170 us
    all_to_all x1, blocking collectives, body(): lax.all_to_all(column_block, 'tok', split_axis=0, concat_axis=1, tiled=True)  98.4 us
    all_gather x1, waiting for transfers between devices, body(): lax.all_gather(stitch_weight, 'tok', axis=0, tiled=True)  91.1 us
    reduce_scatter x1, waiting for transfers between devices, body(): lax.psum_scatter(jnp.dot(context, o_weight, preferred_element_type=jnp.fl...  76 us
    reduce_scatter x1, waiting for transfers between devices, body(): lax.psum_scatter(norm_term.astype(jnp.bfloat16), 'tp', scatter_dimension=...  68.1 us
    all_gather x1, waiting for transfers between devices, body(): gradient_every_row = lax.all_gather(out_grad, 'tp', axis=1, tiled=True)  51.5 us
    all_gather x1, waiting for transfers between devices, body(): gathered = lax.all_gather(source, 'tp', axis=0, tiled=True)  51.3 us
    all_gather x1, waiting for transfers between devices, body(): hidden_all = lax.all_gather(hidden_bf, 'tp', axis=1, tiled=True)  49.4 us
  transfers between devices with their start and end apart: 9, of which 7 were waited for; matrix products, arithmetic and copies ran while one was open for 10% of the time, Pallas kernels for 0%

commit v1 on v0

--- a/solution.py
+++ b/solution.py
@@ -69,7 +69,9 @@
     features = token_rows
     hidden_cols = jnp.dot(
         features,
-        lax.all_gather(stitch_weight, "tok", axis=0, tiled=True),
+        jnp.concatenate(
+            lax.all_to_all(jnp.stack([stitch_weight] * lax.axis_size("tok")), "tok", 0, 0), axis=0
+        ),
         preferred_element_type=jnp.float32,
     )
     hidden_bf = hidden_cols.astype(jnp.bfloat16)

time: 784 us -> 641 us (0.82)
  waiting for transfers between devices: 560 us -> 453 us
  blocking collectives: 98.4 us -> 48.5 us
    all_gather x1 -> x0, waiting for transfers between devices: 91.1 us -> none  [body(): lax.all_gather(stitch_weight, 'tok', axis=0, tiled=True)]
    all_gather x1, waiting for transfers between devices: 51.5 us -> 0.01 us  [body(): gradient_every_row = lax.all_gather(out_grad, 'tp', axis=1, tiled=True)]
    all_to_all x1, blocking collectives: 98.4 us -> 48.5 us  [body(): lax.all_to_all(column_block, 'tok', split_axis=0, concat_axis=1, tiled=True)]
    all_to_all x0 -> x1, waiting for transfers between devices: none -> 33.6 us  [body(): lax.all_to_all(jnp.stack([stitch_weight] * lax.axis_size('tok')), 'tok',...]
    gather x2 -> x1, local copies, waits for them, and re-layouts: 20.1 us -> 13.7 us  [body(): column_block = jnp.take(gathered, placing, axis=0)]
  transfers between devices with their start and end apart: 9 -> 9, of which waited for: 7 -> 6; matrix products, arithmetic and copies ran while one was open for 10% -> 13% of each run, Pallas kernels for 0% -> 0%
where the time goes in v1:
time: 641 us; the launch traced here: 640 us
  waiting for transfers between devices  453 us (71%)
  matrix products  55.6 us (9%)
  blocking collectives  48.5 us (8%)
  local copies, waits for them, and re-layouts  38.3 us (6%)
  other arithmetic  21.7 us (3%)
  between operations  14.5 us (2%)
  starting transfers between devices  8.28 us (1%)
    reduce_scatter x1, waiting for transfers between devices, body(): lax.psum_scatter(lax.dot_general(features, grad_hidden, (((0,), (0,)), ((...  170 us
    reduce_scatter x1, waiting for transfers between devices, body(): lax.psum_scatter(jnp.dot(context, o_weight, preferred_element_type=jnp.fl...  75.9 us
    reduce_scatter x1, waiting for transfers between devices, body(): lax.psum_scatter(norm_term.astype(jnp.bfloat16), 'tp', scatter_dimension=...  61.5 us
    all_gather x1, waiting for transfers between devices, body(): gathered = lax.all_gather(source, 'tp', axis=0, tiled=True)  55.8 us
    all_gather x1, waiting for transfers between devices, body(): hidden_all = lax.all_gather(hidden_bf, 'tp', axis=1, tiled=True)  54.8 us
    all_to_all x1, blocking collectives, body(): lax.all_to_all(column_block, 'tok', split_axis=0, concat_axis=1, tiled=True)  48.5 us
    all_to_all x1, waiting for transfers between devices, body(): lax.all_to_all(jnp.stack([stitch_weight] * lax.axis_size('tok')), 'tok',...  33.6 us
    gather x1, local copies, waits for them, and re-layouts, body(): column_block = jnp.take(gathered, placing, axis=0)  13.7 us
  transfers between devices with their start and end apart: 9, of which 6 were waited for; matrix products, arithmetic and copies ran while one was open for 13% of the time, Pallas kernels for 0%

profile of v1, /device:TPU:1, one launch (start us, length us, event | category | flops | bytes accessed | tf_op | source)
XLA Modules:
  0.0 639.8 jit_solution(16818871389346440461)
XLA Ops:
  7.9 5.2 stack.2
  13.1 6.1 all-to-all-start.1
  20.0 8.0 %scatter_custom_fusion = s32[2048]{0:T(1024)S(1)} fusion(s32[2048]{0:T(1024)S(1)} %compare_select_fusion.1, s32[2048]{0:T(1024)S(1)} %iota.19, s32[]{:T(128)} %constant.22.clone.1), kind=kCustom, calls=%fused_computation.85 | custom fusion | bytes 8196 | tf_op jit(solution)/shard_map/scatter | solution.py:65
  28.1 55.8 %all-gather.4.cloned.1.call-done = bf16[2048,1024]{1,0:T(8,128)(2,1)} async-done(((bf16[128,1024]{1,0:T(8,128)(2,1)}), bf16[2048,1024]{1,0:T(8,128)(2,1)}) %all-gather.4.cloned.1.call-update) | async-done | bytes 4194320 | tf_op jit(solution)/shard_map/all_gather | solution.py:60
  83.9 13.7 %gather_fusion = bf16[2048,1024]{1,0:T(8,128)(2,1)} fusion(bf16[2048,1024]{1,0:T(8,128)(2,1)} %all-gather.4.cloned.1.call-done, s32[2048]{0:T(1024)S(1)} %fusion.44), kind=kCustom, calls=%fused_computation | custom fusion | bytes 8396800 | tf_op jit(solution)/shard_map/jit(_take)/gather | solution.py:67
  97.6 3.9 broadcast_select_fusion
  101.5 33.6 %all-to-all-done.1 = bf16[8,1024,512]{2,1,0:T(8,128)(2,1)} async-done(((bf16[8,1024,512]{2,1,0:T(8,128)(2,1)}), bf16[8,1024,512]{2,1,0:T(8,128)(2,1)}, u32[]{:S(2)}, u32[]{:S(2)}) %all-to-all-start.1) | async-done | bytes 8388640 | tf_op jit(solution)/shard_map/all_to_all | solution.py:73
  135.1 48.5 %all_to_all.21 = bf16[8,256,1024]{2,1,0:T(8,128)(2,1)S(1)} all-to-all(bf16[8,256,1024]{2,1,0:T(8,128)(2,1)} %broadcast_select_fusion), channel_id=1, replica_groups=mesh['tok'=8,'tp'=16] {'tok'}, dimensions={0} | all-to-all | bytes 8388608 | tf_op jit(solution)/shard_map/all_to_all | solution.py:68
  185.6 6.4 %fusion.10 = bf16[256,512]{1,0:T(8,128)(2,1)} fusion(bf16[8,1024,512]{2,1,0:T(8,128)(2,1)} %all-to-all-done.1, bf16[8,256,1024]{2,1,0:T(8,128)(2,1)S(1)} %all_to_all.21), kind=kOutput, calls=%fused_computation.25 | convolution fusion | flops 2147614720 | bytes 12845056 | tf_op jit(solution)/shard_map/dot_general | solution.py:70
  193.5 7.0 %convolution_convert_fusion.3 = bf16[256,512]{1,0:T(8,128)(2,1)S(1)} fusion(bf16[256,8192]{1,0:T(8,128)(2,1)} %all-gather.8.cloned.1.call-done, bf16[512,8192]{1,0:T(8,128)(2,1)} %param.16), kind=kOutput, calls=%fused_computation.26 | convolution fusion | flops 2147614720 | bytes 12845056 | tf_op jit(solution)/shard_map/dot_general | solution.py:136
  201.4 54.8 %all-gather.6.cloned.1.call-done = bf16[256,8192]{1,0:T(8,128)(2,1)} async-done(((bf16[256,512]{1,0:T(8,128)(2,1)}), bf16[256,8192]{1,0:T(8,128)(2,1)}) %all-gather.6.cloned.1.call-update) | async-done | bytes 4194320 | tf_op jit(solution)/shard_map/all_gather | solution.py:78
  256.1 3.3 fusion.1
  259.9 3.9 fusion.13
  264.8 5.8 fusion.11
  280.5 5.9 fusion.55
  286.8 5.3 fusion.7
  292.2 5.9 fusion.6
  298.7 7.7 %convolution_convert_fusion.1 = bf16[256,8192]{1,0:T(8,128)(2,1)} fusion(bf16[256,512]{0,1:T(8,128)(2,1)S(1)} %bitcast.91, bf16[512,8192]{1,0:T(8,128)(2,1)} %param.16), kind=kOutput, calls=%fused_computation.9 | convolution fusion | flops 2149580800 | bytes 12845056 | tf_op jit(solution)/shard_map/dot_general | solution.py:129
  306.5 6.6 %copy.31 = bf16[256,8,1024]{0,2,1:T(8,128)(2,1)} copy(bf16[256,8,1024]{2,0,1:T(8,128)(2,1)} %bitcast.89) | data formatting | bytes 8388608 | tf_op jit(solution)/shard_map/all_to_all | solution.py:68
  313.1 61.5 %reduce-scatter.6.cloned.1.call-done = bf16[256,512]{1,0:T(8,128)(2,1)} async-done(((bf16[256,8192]{1,0:T(8,128)(2,1)}), bf16[256,512]{1,0:T(8,128)(2,1)}) %reduce-scatter.6.cloned.1.call-update) | async-done | bytes 262160 | tf_op jit(solution)/shard_map/reduce_scatter | solution.py:177
  374.6 7.9 %convolution_convert_fusion = bf16[8192,512]{1,0:T(8,128)(2,1)} fusion(bf16[256,8192]{0,1:T(8,128)(2,1)} %bitcast.87, bf16[256,512]{1,0:T(8,128)(2,1)} %reduce-scatter.6.cloned.1.call-done, bf16[256,512]{1,0:T(8,128)(2,1)S(1)} %copy-done.4), kind=kOutput, calls=%fused_computation.6 | convolution fusion | flops 2152202240 | bytes 13107200 | tf_op jit(solution)/shard_map/dot_general | solution.py:183
  382.6 75.9 %reduce-scatter.4.cloned.1.call-done = bf16[256,512]{1,0:T(8,128)(2,1)} async-done(((bf16[256,8192]{1,0:T(8,128)(2,1)}), bf16[256,512]{1,0:T(8,128)(2,1)}) %reduce-scatter.4.cloned.1.call-update) | async-done | bytes 262160 | tf_op jit(solution)/shard_map/reduce_scatter | solution.py:128
  460.2 169.9 %reduce-scatter.8.cloned.1.call-done = bf16[1024,512]{1,0:T(8,128)(2,1)} async-done(((bf16[8192,512]{1,0:T(8,128)(2,1)}), bf16[1024,512]{1,0:T(8,128)(2,1)}) %reduce-scatter.8.cloned.1.call-update) | async-done | bytes 1048592 | tf_op jit(solution)/shard_map/reduce_scatter | solution.py:182
  630.1 2.8 convert_element_type.137
  (90 shorter events, 19.8 us)
Async XLA Ops:
  7.2 252.8 %copy-start = (bf16[8192,128]{1,0:T(8,128)(2,1)S(1)}, bf16[8192,128]{1,0:T(8,128)(2,1)}, u32[]{:S(2)}) copy-start(bf16[8192,128]{1,0:T(8,128)(2,1)} %param.15) | copy-start | bytes 6291460
  7.2 76.7 %all-gather.4.cloned.1.call-start = ((), (), s32[]{:S(2)}) async-start(), calls=%async_computation.5 | async-start | bytes 4456448 | tf_op jit(solution)/shard_map/all_gather | solution.py:60
  13.1 6.9 %copy-start.15 = (s32[2048]{0:T(1024)S(1)}, s32[2048]{0:T(1024)}, u32[]{:S(2)}) copy-start(s32[2048]{0:T(1024)} %param.10) | copy-start | bytes 24580
  13.1 122.0 %all-to-all-start.1 = ((bf16[8,1024,512]{2,1,0:T(8,128)(2,1)}), bf16[8,1024,512]{2,1,0:T(8,128)(2,1)}, u32[]{:S(2)}, u32[]{:S(2)}) async-start(bf16[8,1024,512]{2,1,0:T(8,128)(2,1)} %stack.2), calls=%async_computation.1 | async-start | bytes 16777216 | tf_op jit(solution)/shard_map/all_to_all | solution.py:73
  19.2 174.3 %all-gather.8.cloned.1.call-start = ((), (), s32[]{:S(2)}) async-start(), calls=%async_computation.8 | async-start | bytes 4456448 | tf_op jit(solution)/shard_map/all_gather | solution.py:135
  19.9 236.2 %all-gather.6.cloned.1.call-start = ((), (), s32[]{:S(2)}) async-start(), calls=%async_computation.6 | async-start | bytes 4456448 | tf_op jit(solution)/shard_map/all_gather | solution.py:78
  185.6 6.5 %copy-start.14 = (s32[1,256]{1,0:T(1,128)S(1)}, s32[1,256]{1,0:T(1,128)}, u32[]{:S(2)}) copy-start(s32[1,256]{1,0:T(1,128)} %param.11) | copy-start | bytes 3076
  192.0 182.6 %reduce-scatter.6.cloned.1.call-start = ((), (), s32[]{:S(2)}) async-start(), calls=%async_computation.9 | async-start | bytes 4456448 | tf_op jit(solution)/shard_map/reduce_scatter | solution.py:177
  193.5 66.5 %copy-start.12 = (f32[8192]{0:T(1024)S(1)}, f32[8192]{0:T(1024)}, u32[]{:S(2)}) copy-start(f32[8192]{0:T(1024)} %param.13) | copy-start | bytes 98308
  256.1 8.6 %copy-start.1 = (bf16[256,8192]{1,0:T(8,128)(2,1)S(1)}, bf16[256,8192]{1,0:T(8,128)(2,1)}, u32[]{:S(2)}) copy-start(bf16[256,8192]{1,0:T(8,128)(2,1)} %all-gather.6.cloned.1.call-done) | copy-start | bytes 12582916
  259.9 10.7 %copy-start.17 = (f32[256]{0:T(256)}, f32[256]{0:T(256)S(1)}, u32[]{:S(2)}) copy-start(f32[256]{0:T(256)S(1)} %get-tuple-element.15) | copy-start | bytes 3076
  264.2 10.5 %copy-start.6 = (bf16[256,128]{0,1:T(8,128)(2,1)}, bf16[256,128]{0,1:T(8,128)(2,1)S(1)}, u32[]{:S(2)}) copy-start(bf16[256,128]{0,1:T(8,128)(2,1)S(1)} %fusion.23) | copy-start | bytes 196612
  264.2 7.1 %collective-permute-start = (bf16[256,128]{0,1:T(8,128)(2,1)S(1)}, bf16[256,128]{0,1:T(8,128)(2,1)S(1)}, u32[]{:S(2)}, u32[]{:S(2)}) collective-permute-start(bf16[256,128]{0,1:T(8,128)(2,1)S(1)} %fusion.23), channel_id=1, source_target_pairs={{0,1},{1,0},{2,3},{3,2},{4,5},{5,4},{6,7},{7,6},{8,9},{9,8},{10,11... | collective-permute-start | bytes 196616 | tf_op jit(solution)/shard_map/ppermute | solution.py:14
  279.2 7.2 %collective-permute-start.1 = (bf16[256,128]{0,1:T(8,128)(2,1)S(1)}, bf16[256,128]{0,1:T(8,128)(2,1)S(1)}, u32[]{:S(2)}, u32[]{:S(2)}) collective-permute-start(bf16[256,128]{0,1:T(8,128)(2,1)S(1)} %fusion.37), channel_id=1, source_target_pairs={{0,1},{1,0},{2,3},{3,2},{4,5},{5,4},{6,7},{7,6},{8,9},{9,8},{10,11... | collective-permute-start | bytes 196616 | tf_op jit(solution)/shard_map/ppermute | solution.py:14
  280.5 6.0 copy-start.8
  280.5 6.3 copy-start.2
  280.5 6.3 copy-start.13
  286.8 5.3 copy-start.16
  292.1 6.2 copy-start.7
  292.2 6.2 copy-start.11
  298.0 160.5 %reduce-scatter.4.cloned.1.call-start = ((), (), s32[]{:S(2)}) async-start(), calls=%async_computation.7 | async-start | bytes 4456448 | tf_op jit(solution)/shard_map/reduce_scatter | solution.py:128
  306.4 68.3 %copy-start.4 = (bf16[256,512]{1,0:T(8,128)(2,1)S(1)}, bf16[256,512]{1,0:T(8,128)(2,1)}, u32[]{:S(2)}) copy-start(bf16[256,512]{1,0:T(8,128)(2,1)} %param.17) | copy-start | bytes 786436
  306.4 323.7 %reduce-scatter.8.cloned.1.call-start = ((), (), s32[]{:S(2)}) async-start(), calls=%async_computation.10 | async-start | bytes 9437184 | tf_op jit(solution)/shard_map/reduce_scatter | solution.py:182
  374.6 83.9 %copy-start.5 = (bf16[256,512]{1,0:T(8,128)(2,1)S(1)}, bf16[256,512]{1,0:T(8,128)(2,1)}, u32[]{:S(2)}) copy-start(bf16[256,512]{1,0:T(8,128)(2,1)} %fusion.10) | copy-start | bytes 786436
  (4 other events, 15.0 us)
Sparse Core Ops, SparseCore 0:
  10.5 73.3 all-gather.3
  86.3 66.0 all-gather.7
  192.1 63.9 all-gather.5
  298.2 76.4 reduce-scatter.5
  379.0 79.4 reduce-scatter.3
  460.8 169.3 reduce-scatter.7
